TPU v7x, 256 devices: a whole 4x4x8 slice. The times are simulated.
256 devices in a mesh: orb: 8 (over y, core), aux: 32 (over x, z).
Axes of the slice: x: 4, y: 4, z: 8, core: 2. Of those that a mesh axis runs over, the one named last changes fastest.
Arguments:
- factors: bfloat16 [384, 128, 2048], P('orb', None, 'aux'), may hold values from -6 to 6
- amplitudes: bfloat16 [384, 12, 128, 128], P('orb'), may hold values from -0.15625 to 0.15625
- partners: int32 [384, 12], P('orb'), may hold values from 0 to 383, as said below
- metric_tiles: bfloat16 [128, 128, 128], P('aux'), may hold values from -0.1875 to 0.1875
- tile_pos: int32 [128, 2], P('aux'), may hold values from 0 to 15, as said below
Outputs:
- density: bfloat16 [384, 128, 2048], P('orb', 'aux')
Inputs may be any that keep to these rules, and one draw needn't show every extreme that they name: partners[i, 0] = i for every orbital i; the other partners of an orbital are any orbitals, repeats allowed. `tile_pos`: the listed positions (row block, column block) are all distinct, and each of the 16 diagonal positions is listed.
All inputs are finite; a program needn't handle non-finite values.
Results may differ from a plain program's by a relative error of at most 0.0049.
Values may be sent and summed in bfloat16 or wider, within the bound.
A program may use at most 128 MiB of HBM per device.

v0:
```python
import jax
import jax.numpy as jnp
from jax import lax
from jax.sharding import PartitionSpec as P


def placed_terms(tile_set, positions, block_count):
    levels = jnp.arange(block_count, dtype=jnp.int32)
    row_hits = (positions[:, 0:1] == levels[None, :]).astype(jnp.bfloat16)
    col_hits = (positions[:, 1:2] == levels[None, :]).astype(jnp.bfloat16)
    pair_table = (row_hits[:, :, None] * col_hits[:, None, :]).reshape(
        tile_set.shape[0], block_count * block_count
    )
    flat_tiles = tile_set.reshape(tile_set.shape[0], tile_set.shape[1] * tile_set.shape[2])
    return lax.dot_general(
        pair_table, flat_tiles, (((0,), (0,)), ((), ())), preferred_element_type=jnp.float32
    )


def apply_metric(row_block, placed, block_count, span):
    blocks = placed.astype(jnp.bfloat16).reshape(block_count, block_count, span, span)
    rows_split = row_block.reshape(row_block.shape[0], block_count, span)
    result = jnp.einsum("ars,rcsu->acu", rows_split, blocks, preferred_element_type=jnp.float32)
    return result.reshape(row_block.shape[0], block_count * span)


def shards(factors, amplitudes, partners, metric_tiles, tile_pos):
    group_size, domain, aux_part = factors.shape
    flat_factors = factors.reshape(group_size, domain * aux_part)
    gathered = lax.all_gather(flat_factors, "orb", axis=0, tiled=True)
    picked = jnp.take(gathered, partners.reshape(-1), axis=0)
    picked = picked.reshape(partners.shape[0], partners.shape[1], domain, aux_part)
    gammas = jnp.einsum("ikab,ikbp->iap", amplitudes, picked, preferred_element_type=jnp.float32)
    gammas = gammas.astype(jnp.bfloat16)
    owned_rows = lax.all_to_all(gammas, "aux", split_axis=1, concat_axis=2, tiled=True)
    row_block = owned_rows.reshape(owned_rows.shape[0] * owned_rows.shape[1], owned_rows.shape[2])
    span = metric_tiles.shape[1]
    block_count = row_block.shape[1] // span
    placed = placed_terms(
        lax.all_gather(metric_tiles, "aux", axis=0, tiled=True),
        lax.all_gather(tile_pos, "aux", axis=0, tiled=True),
        block_count,
    )
    result = apply_metric(row_block, placed, block_count, span)
    return result.reshape(owned_rows.shape).astype(jnp.bfloat16)


def solution(mesh):
    in_specs = (
        P("orb", None, "aux"),
        P("orb", None, None, None),
        P("orb", None),
        P("aux", None, None),
        P("aux", None),
    )
    out_specs = P("orb", "aux", None)
    return jax.shard_map(shards, mesh=mesh, in_specs=in_specs, out_specs=out_specs, check_vma=False)
```

profile of v0, /device:TPU:24, one launch (start us, length us, event | category | flops | bytes accessed | tf_op | source)
XLA Modules:
  0.0 204.2 jit_solution(7695285728470506883)
XLA Ops:
  6.5 0.0 all-gather.4.cloned.1.call-start
  6.5 1.8 copy.22
  8.3 2.1 %reshape.111 = bf16[48,8192]{1,0:T(8,128)(2,1)} reshape(bf16[48,128,64]{2,1,0:T(8,128)(2,1)S(1)} %copy.22) | data formatting | bytes 1572864 | tf_op jit(solution)/shard_map/reshape | solution.py:29
  10.4 0.0 all-gather.4.cloned.1.call-update
  10.4 0.0 all-gather.6.cloned.1.call-start
  10.4 0.7 all-gather.6.cloned.1.call-update
  11.2 46.1 %all-gather = s32[32,4,2]{1,2,0:T(2,128)S(1)} all-gather(s32[1,4,2]{1,2,0:T(2,128)} %bitcast.51), channel_id=1, replica_groups=mesh['orb'=8,'aux'=32] {'aux'}, dimensions={0}, use_global_device_ids=true | all-gather | bytes 1056 | tf_op jit(solution)/shard_map/all_gather | solution.py:41
  57.2 0.1 reshape.124
  57.3 0.8 copy.23
  58.1 0.1 reshape.112
  58.2 0.7 compare_and_fusion
  58.9 0.1 copy.21
  59.1 0.0 all-gather.4.cloned.1.call-done
  59.1 24.6 %gather_fusion = bf16[576,8192]{1,0:T(8,128)(2,1)} fusion(bf16[384,8192]{1,0:T(8,128)(2,1)} %all-gather.4.cloned.1.call-done, s32[1024]{0:T(1024)S(1)} %pad_clamp_fusion), kind=kCustom, calls=%fused_computation | custom fusion | bytes 18876672 | tf_op jit(solution)/shard_map/jit(_take)/gather | solution.py:31
  83.7 26.1 %gather.7 = bf16[48,12,128,64]{3,2,1,0:T(8,128)(2,1)} reshape(bf16[576,8192]{1,0:T(8,128)(2,1)} %gather_fusion) | data formatting | bytes 18874368 | tf_op jit(solution)/shard_map/jit(_take)/gather | solution.py:31
  109.9 14.9 %fusion.10 = bf16[48,128,64]{1,2,0:T(8,128)(2,1)S(1)} fusion(bf16[48,12,128,128]{3,2,1,0:T(8,128)(2,1)} %param.6, bf16[48,12,128,64]{3,2,1,0:T(8,128)(2,1)} %gather.7, pred[48,12]{1,0:T(8,128)(4,1)S(1)} %copy.21), kind=kOutput, calls=%fused_computation.13 | convolution fusion | flops 1213071360 | bytes 29098560 | tf_op jit(solution)/shard_map/ikab,ikbp->iap/dot_general | solution.py:33
  124.7 1.0 copy.25
  125.7 1.9 reshape.129
  127.6 6.6 %all-to-all-start = ((bf16[32,2,6144]{2,1,0:T(2,128)(2,1)}), bf16[32,2,6144]{2,1,0:T(2,128)(2,1)S(1)}, u32[]{:S(2)}, u32[]{:S(2)}) async-start(bf16[32,2,6144]{2,1,0:T(2,128)(2,1)} %reshape.129), calls=%async_computation | async-start | bytes 1572864 | tf_op jit(solution)/shard_map/all_to_all | solution.py:35
  134.2 11.8 %all-gather.6.cloned.1.call-done = bf16[128,128,128]{2,1,0:T(8,128)(2,1)} async-done(((bf16[4,128,128]{2,1,0:T(8,128)(2,1)}), bf16[128,128,128]{2,1,0:T(8,128)(2,1)}) %all-gather.6.cloned.1.call-update) | async-done | bytes 4194320 | tf_op jit(solution)/shard_map/all_gather | solution.py:40
  146.1 8.8 %fusion.4 = bf16[32,8,128,128]{3,1,2,0:T(8,128)(2,1)} fusion(bf16[128,256]{0,1:T(8,128)(2,1)S(1)} %bitcast.50, bf16[16,8,128,128]{3,2,1,0:T(8,128)(2,1)} %bitcast.49), kind=kOutput, calls=%fused_computation.7 | convolution fusion | flops 1077936128 | bytes 12648448 | tf_op jit(solution)/shard_map/dot_general | solution.py:15
  154.9 9.2 %copy.35 = bf16[32,8,128,128]{3,2,1,0:T(8,128)(2,1)} copy(bf16[32,8,128,128]{3,1,2,0:T(8,128)(2,1)} %fusion.4) | data formatting | bytes 16777216
  164.1 10.4 %bitcast_bitcast_fusion = bf16[16,128,16,128]{1,3,0,2:T(8,128)(2,1)} fusion(bf16[16,16,128,128]{3,2,1,0:T(8,128)(2,1)} %bitcast.45), kind=kLoop, calls=%fused_computation.6 | loop fusion | bytes 16777216 | tf_op jit(solution)/shard_map/ars,rcsu->acu/dot_general | solution.py:23
  174.4 12.3 %copy.28 = bf16[16,128,16,128]{3,1,0,2:T(8,128)(2,1)} copy(bf16[16,128,16,128]{1,3,0,2:T(8,128)(2,1)} %bitcast_bitcast_fusion) | data formatting | bytes 16777216 | tf_op jit(solution)/shard_map/ars,rcsu->acu/dot_general | solution.py:23
  186.7 0.0 all-to-all-done
  186.8 1.0 reshape.130
  187.8 1.0 copy.26
  188.8 0.7 dot_general.16
  189.5 6.3 %fusion.7 = bf16[48,4,2048]{2,0,1:T(8,128)(2,1)S(1)} fusion(bf16[2048,16,128,1]{2,0,1,3:T(8,128)(2,1)} %bitcast.46, bf16[48,4,16,128]{3,2,1,0:T(8,128)(2,1)S(1)} %dot_general.16), kind=kOutput, calls=%fused_computation.11 | convolution fusion | flops 1611005952 | bytes 9961472 | tf_op jit(solution)/shard_map/ars,rcsu->acu/dot_general | solution.py:23
  195.9 1.5 copy.30
  (6 shorter events, 0.0 us)
Async XLA Ops:
  6.5 52.6 %all-gather.4.cloned.1.call-start = ((), (), s32[]{:S(2)}) async-start(), calls=%async_computation.1 | async-start | bytes 7077888 | tf_op jit(solution)/shard_map/all_gather | solution.py:30
  10.4 135.7 %all-gather.6.cloned.1.call-start = ((), (), s32[]{:S(2)}) async-start(), calls=%async_computation.2 | async-start | bytes 4325376 | tf_op jit(solution)/shard_map/all_gather | solution.py:40
  127.6 59.2 %all-to-all-start = ((bf16[32,2,6144]{2,1,0:T(2,128)(2,1)}), bf16[32,2,6144]{2,1,0:T(2,128)(2,1)S(1)}, u32[]{:S(2)}, u32[]{:S(2)}) async-start(bf16[32,2,6144]{2,1,0:T(2,128)(2,1)} %reshape.129), calls=%async_computation | async-start | bytes 1572864 | tf_op jit(solution)/shard_map/all_to_all | solution.py:35
Sparse Core Ops, SparseCore 0:
  10.5 44.1 all-gather.3
  57.4 88.6 all-gather.5
where the time goes:
time: 206 us; the launch traced here: 204 us
  local copies, waits for them, and re-layouts  94.6 us (46%)
  blocking collectives  46.1 us (22%)
  matrix products  30 us (15%)
  between operations  13.5 us (7%)
  waiting for transfers between devices  12.6 us (6%)
  starting transfers between devices  6.66 us (3%)
    gather x2, local copies, waits for them, and re-layouts, shards(): picked = jnp.take(gathered, partners.reshape(-1), axis=0)  50.7 us
    all_gather x1, blocking collectives, shards(): lax.all_gather(tile_pos, 'aux', axis=0, tiled=True)  46.1 us
    dot_general x3, local copies, waits for them, and re-layouts, apply_metric(): jnp.einsum('ars,rcsu->acu', rows_split, blocks, preferred_element_type=jn...  23.4 us
    dot_general x1, matrix products, shards(): jnp.einsum('ikab,ikbp->iap', amplitudes, picked, preferred_element_type=j...  14.9 us
    unnamed x6, local copies, waits for them, and re-layouts  14.7 us
    all_gather x1, waiting for transfers between devices, shards(): lax.all_gather(metric_tiles, 'aux', axis=0, tiled=True)  11.8 us
    dot_general x1, matrix products, placed_terms(): lax.dot_general(pair_table, flat_tiles, (((0,), (0,)), ((), ())), preferr...  8.82 us
    all_to_all x1, starting transfers between devices, shards(): lax.all_to_all(gammas, 'aux', split_axis=1, concat_axis=2, tiled=True)  6.62 us
  transfers between devices with their start and end apart: 3, of which 1 were waited for; matrix products, arithmetic and copies ran while one was open for 54% of the time, Pallas kernels for 0%

commit v1 on v0

--- a/solution.py
+++ b/solution.py
@@ -37,7 +37,9 @@
     span = metric_tiles.shape[1]
     block_count = row_block.shape[1] // span
     placed = placed_terms(
-        lax.all_gather(metric_tiles, "aux", axis=0, tiled=True),
+        jnp.concatenate(
+            lax.all_to_all(jnp.stack([metric_tiles] * lax.axis_size("aux")), "aux", 0, 0), axis=0
+        ),
         lax.all_gather(tile_pos, "aux", axis=0, tiled=True),
         block_count,
     )

time: 206 us -> 289 us (1.40)
  blocking collectives: 46.1 us -> 128 us
  waiting for transfers between devices: 12.6 us -> 0.04 us
  starting transfers between devices: 6.66 us -> 18.4 us
  local copies, waits for them, and re-layouts: 94.6 us -> 97.9 us
    all_gather x1, blocking collectives: 46.1 us -> 128 us  [shards(): lax.all_gather(tile_pos, 'aux', axis=0, tiled=True)]
    all_gather x1 -> x0, waiting for transfers between devices: 11.8 us -> none  [shards(): lax.all_gather(metric_tiles, 'aux', axis=0, tiled=True)]
    all_to_all x0 -> x1, starting transfers between devices: none -> 11.4 us  [shards(): lax.all_to_all(jnp.stack([metric_tiles] * lax.axis_size('aux')), 'aux', 0...]
    another operation x0 -> x1, local copies, waits for them, and re-layouts: none -> 3.93 us  [shards(): jnp.stack([metric_tiles] * lax.axis_size('aux'))]
    unnamed x6 -> x10, local copies, waits for them, and re-layouts: 14.7 us -> 14.1 us
  transfers between devices with their start and end apart: 3 -> 3, of which waited for: 1 -> 0; matrix products, arithmetic and copies ran while one was open for 54% -> 39% of each run, Pallas kernels for 0% -> 0%
where the time goes in v1:
time: 289 us; the launch traced here: 288 us
  blocking collectives  128 us (44%)
  local copies, waits for them, and re-layouts  97.9 us (34%)
  matrix products  29.7 us (10%)
  starting transfers between devices  18.4 us (6%)
  between operations  13.5 us (5%)
    all_gather x1, blocking collectives, shards(): lax.all_gather(tile_pos, 'aux', axis=0, tiled=True)  128 us
    gather x2, local copies, waits for them, and re-layouts, shards(): picked = jnp.take(gathered, partners.reshape(-1), axis=0)  50.7 us
    dot_general x3, local copies, waits for them, and re-layouts, apply_metric(): jnp.einsum('ars,rcsu->acu', rows_split, blocks, preferred_element_type=jn...  23.4 us
    dot_general x1, matrix products, shards(): jnp.einsum('ikab,ikbp->iap', amplitudes, picked, preferred_element_type=j...  14.6 us
    unnamed x10, local copies, waits for them, and re-layouts  14.1 us
    all_to_all x1, starting transfers between devices, shards(): lax.all_to_all(jnp.stack([metric_tiles] * lax.axis_size('aux')), 'aux', 0...  11.4 us
    dot_general x1, matrix products, placed_terms(): lax.dot_general(pair_table, flat_tiles, (((0,), (0,)), ((), ())), preferr...  8.8 us
    all_to_all x1, starting transfers between devices, shards(): lax.all_to_all(gammas, 'aux', split_axis=1, concat_axis=2, tiled=True)  6.99 us
  transfers between devices with their start and end apart: 3, of which 0 were waited for; matrix products, arithmetic and copies ran while one was open for 39% of the time, Pallas kernels for 0%

profile of v1, /device:TPU:24, one launch (start us, length us, event | category | flops | bytes accessed | tf_op | source)
XLA Modules:
  0.0 287.6 jit_solution(15477783738014289195)
XLA Ops:
  6.5 0.0 all-gather.3.cloned.1.call-start
  6.5 1.8 copy.22
  8.3 0.0 copy-start.1
  8.3 0.0 copy-start
  8.3 2.1 reshape.110
  10.4 0.0 all-gather.3.cloned.1.call-update
  10.4 3.9 %stack.2 = bf16[32,4,128,128]{3,2,1,0:T(8,128)(2,1)} broadcast(bf16[4,128,128]{2,1,0:T(8,128)(2,1)} %param.8), dimensions={1,2,3} | broadcast | bytes 4325376 | tf_op jit(solution)/shard_map/stack | solution.py:41
  14.4 11.4 %all-to-all-start.1 = ((bf16[32,4,128,128]{3,2,1,0:T(8,128)(2,1)}), bf16[32,4,128,128]{3,2,1,0:T(8,128)(2,1)}, u32[]{:S(2)}, u32[]{:S(2)}) async-start(bf16[32,4,128,128]{3,2,1,0:T(8,128)(2,1)} %stack.2), calls=%async_computation.1 | async-start | bytes 8388608 | tf_op jit(solution)/shard_map/all_to_all | solution.py:41
  25.8 0.0 copy-done.1
  25.8 127.9 %all-gather = s32[32,4,2]{1,2,0:T(2,128)S(1)} all-gather(s32[1,4,2]{1,2,0:T(2,128)S(1)} %bitcast.51), channel_id=1, replica_groups=mesh['orb'=8,'aux'=32] {'aux'}, dimensions={0}, use_global_device_ids=true | all-gather | bytes 1056 | tf_op jit(solution)/shard_map/all_gather | solution.py:43
  153.8 0.1 reshape.122
  153.9 0.0 copy-done
  153.9 0.1 copy.23
  154.0 0.1 reshape.111
  154.1 0.1 copy.21
  154.3 0.0 all-gather.3.cloned.1.call-done
  154.3 24.6 %gather_fusion = bf16[576,8192]{1,0:T(8,128)(2,1)} fusion(bf16[384,8192]{1,0:T(8,128)(2,1)} %all-gather.3.cloned.1.call-done, s32[1024]{0:T(1024)S(1)} %pad_clamp_fusion), kind=kCustom, calls=%fused_computation | custom fusion | bytes 18876672 | tf_op jit(solution)/shard_map/jit(_take)/gather | solution.py:31
  178.9 26.1 %gather.7 = bf16[48,12,128,64]{3,2,1,0:T(8,128)(2,1)} reshape(bf16[576,8192]{1,0:T(8,128)(2,1)} %gather_fusion) | data formatting | bytes 18874368 | tf_op jit(solution)/shard_map/jit(_take)/gather | solution.py:31
  205.0 14.6 %fusion.10 = bf16[48,128,64]{1,2,0:T(8,128)(2,1)S(1)} fusion(bf16[48,12,128,128]{3,2,1,0:T(8,128)(2,1)} %param.6, bf16[48,12,128,64]{3,2,1,0:T(8,128)(2,1)} %gather.7, pred[48,12]{1,0:T(8,128)(4,1)S(1)} %copy.21), kind=kOutput, calls=%fused_computation.13 | convolution fusion | flops 1213071360 | bytes 29098560 | tf_op jit(solution)/shard_map/ikab,ikbp->iap/dot_general | solution.py:33
  219.6 1.0 copy.25
  220.6 1.9 reshape.127
  222.5 0.0 all-to-all-done.1
  222.5 7.0 %all-to-all-start = ((bf16[32,2,6144]{2,1,0:T(2,128)(2,1)}), bf16[32,2,6144]{2,1,0:T(2,128)(2,1)S(1)}, u32[]{:S(2)}, u32[]{:S(2)}) async-start(bf16[32,2,6144]{2,1,0:T(2,128)(2,1)} %reshape.127), calls=%async_computation | async-start | bytes 1572864 | tf_op jit(solution)/shard_map/all_to_all | solution.py:35
  229.5 8.8 %fusion.4 = bf16[32,8,128,128]{3,1,2,0:T(8,128)(2,1)} fusion(bf16[128,256]{0,1:T(8,128)(2,1)S(1)} %bitcast.50, bf16[16,8,128,128]{3,2,1,0:T(8,128)(2,1)} %bitcast.19), kind=kOutput, calls=%fused_computation.7 | convolution fusion | flops 1077936128 | bytes 12648448 | tf_op jit(solution)/shard_map/dot_general | solution.py:15
  238.3 9.2 %copy.35 = bf16[32,8,128,128]{3,2,1,0:T(8,128)(2,1)} copy(bf16[32,8,128,128]{3,1,2,0:T(8,128)(2,1)} %fusion.4) | data formatting | bytes 16777216
  247.5 10.3 %bitcast_bitcast_fusion = bf16[16,128,16,128]{1,3,0,2:T(8,128)(2,1)} fusion(bf16[16,16,128,128]{3,2,1,0:T(8,128)(2,1)} %bitcast.46), kind=kLoop, calls=%fused_computation.6 | loop fusion | bytes 16777216 | tf_op jit(solution)/shard_map/ars,rcsu->acu/dot_general | solution.py:23
  257.9 12.3 %copy.28 = bf16[16,128,16,128]{3,1,0,2:T(8,128)(2,1)} copy(bf16[16,128,16,128]{1,3,0,2:T(8,128)(2,1)} %bitcast_bitcast_fusion) | data formatting | bytes 16777216 | tf_op jit(solution)/shard_map/ars,rcsu->acu/dot_general | solution.py:23
  270.2 0.0 all-to-all-done
  270.2 1.0 reshape.128
  271.2 1.0 copy.26
  272.2 0.7 dot_general.16
  273.0 6.3 %fusion.7 = bf16[48,4,2048]{2,0,1:T(8,128)(2,1)S(1)} fusion(bf16[2048,16,128,1]{2,0,1,3:T(8,128)(2,1)} %bitcast.47, bf16[48,4,16,128]{3,2,1,0:T(8,128)(2,1)S(1)} %dot_general.16), kind=kOutput, calls=%fused_computation.11 | convolution fusion | flops 1611005952 | bytes 9961472 | tf_op jit(solution)/shard_map/ars,rcsu->acu/dot_general | solution.py:23
  279.3 1.5 copy.30
  (7 shorter events, 0.1 us)
Async XLA Ops:
  6.5 147.8 %all-gather.3.cloned.1.call-start = ((), (), s32[]{:S(2)}) async-start(), calls=%async_computation.2 | async-start | bytes 7077888 | tf_op jit(solution)/shard_map/all_gather | solution.py:30
  8.3 17.5 %copy-start.1 = (s32[4,2]{0,1:T(2,128)S(1)}, s32[4,2]{0,1:T(2,128)}, u32[]{:S(2)}) copy-start(s32[4,2]{0,1:T(2,128)} %param.9) | copy-start | bytes 100
  8.3 145.6 %copy-start = (s32[48,12]{0,1:T(8,128)S(1)}, s32[48,12]{0,1:T(8,128)}, u32[]{:S(2)}) copy-start(s32[48,12]{0,1:T(8,128)} %param.7) | copy-start | bytes 6916
  14.4 208.1 %all-to-all-start.1 = ((bf16[32,4,128,128]{3,2,1,0:T(8,128)(2,1)}), bf16[32,4,128,128]{3,2,1,0:T(8,128)(2,1)}, u32[]{:S(2)}, u32[]{:S(2)}) async-start(bf16[32,4,128,128]{3,2,1,0:T(8,128)(2,1)} %stack.2), calls=%async_computation.1 | async-start | bytes 8388608 | tf_op jit(solution)/shard_map/all_to_all | solution.py:41
  222.5 47.7 %all-to-all-start = ((bf16[32,2,6144]{2,1,0:T(2,128)(2,1)}), bf16[32,2,6144]{2,1,0:T(2,128)(2,1)S(1)}, u32[]{:S(2)}, u32[]{:S(2)}) async-start(bf16[32,2,6144]{2,1,0:T(2,128)(2,1)} %reshape.127), calls=%async_computation | async-start | bytes 1572864 | tf_op jit(solution)/shard_map/all_to_all | solution.py:35
Sparse Core Ops, SparseCore 0:
  10.5 44.1 all-gather.2
